TPU v7x, 512 devices: a whole 4x8x8 slice. The times are simulated.
512 devices in a mesh: feat: 128 (over y, x, z_lo, core), layer: 4 (over z_hi).
Axes of the slice: x: 4, y: 8, z: 8 (z_hi: 4, z_lo: 2; z = z_hi * 2 + z_lo), core: 2. Of those that a mesh axis runs over, the one named last changes fastest.
Arguments:
- residual_in: bfloat16 [4, 384, 2304], P('layer', 'feat'), as said below
- enc_weight: bfloat16 [4, 2304, 8192], P('layer', None, 'feat'), as said below
- thresholds: int32 [4, 8192], P('layer', 'feat'), may hold values from -2016 to 7341, as said below
- dec_weight: bfloat16 [4, 4, 8192, 2304], P(None, 'layer', 'feat'), may hold values from -0.03125 to 0.03125
- target: bfloat16 [4, 384, 2304], P('layer', 'feat')
Outputs:
- loss_value: float32 [], replicated
- reconstruction: bfloat16 [4, 384, 2304], P('layer', 'feat')
- dec_grad: bfloat16 [4, 4, 8192, 2304], P(None, 'layer', 'feat')
- enc_grad: bfloat16 [4, 2304, 8192], P('layer', None, 'feat')
Inputs may be any that keep to these rules, and one draw needn't show every extreme that they name: `residual_in`: every entry is a multiple of 1/8. `enc_weight`: every entry is a multiple of 1/256. `thresholds`: whole numbers.
All inputs are finite; a program needn't handle non-finite values.
Results may differ from a plain program's by a relative error of at most 0.007.
Values may be sent and summed in bfloat16 or wider, within the bound.
A program may use at most 64 MiB of HBM per device.

v0:
```python
import jax
import jax.numpy as jnp
from jax import lax
from jax.sharding import PartitionSpec as P

ERROR_SCALE = 32.0
PENALTY_WEIGHT = 4.0


def body(residual_in, enc_weight, thresholds, dec_weight, target):
    local_rows = residual_in[0]
    encoder = enc_weight[0]
    jump_level = (thresholds[0].astype(jnp.float32) + 0.5) / 2048.0
    preactivation = jnp.dot(
        lax.all_gather(local_rows, "feat", axis=0, tiled=True),
        encoder,
        preferred_element_type=jnp.float32,
    )
    active_mask = preactivation > jump_level[None, :]
    layer_activations = jnp.where(active_mask, preactivation, 0.0).astype(jnp.bfloat16)
    token_count = preactivation.shape[0]
    magnitude = jnp.mean(jnp.abs(layer_activations.astype(jnp.float32)), axis=0)
    penalty_local = jnp.sum(magnitude * magnitude)
    penalty_total = lax.psum(penalty_local, ("feat", "layer"))
    all_acts = lax.all_gather(layer_activations[None], "layer", axis=0, tiled=True)
    decoder = dec_weight[:, 0]
    recon = lax.psum_scatter(
        jnp.einsum("sif,sfd->id", all_acts, decoder, preferred_element_type=jnp.float32),
        "feat",
        scatter_dimension=0,
        tiled=True,
    )
    error_rows = recon - target[0].astype(jnp.float32)
    grad_local = (error_rows / ERROR_SCALE).astype(jnp.bfloat16)
    grad_all = lax.all_gather(grad_local, "feat", axis=0, tiled=True)
    squares_local = jnp.sum(error_rows * error_rows)
    squares_total = lax.psum(squares_local, ("feat", "layer"))
    dec_grad = jnp.einsum(
        "sif,id->sfd", all_acts, grad_all, preferred_element_type=jnp.float32
    ).astype(jnp.bfloat16)
    act_part = jnp.einsum("id,sfd->sif", grad_all, decoder, preferred_element_type=jnp.float32)
    activation_gradient = lax.psum_scatter(act_part, "layer", scatter_dimension=0, tiled=True)[0]
    sparsity_gradient = (
        2.0
        * PENALTY_WEIGHT
        * magnitude[None, :]
        * jnp.sign(layer_activations.astype(jnp.float32))
        / token_count
    )
    preactivation_gradient = jnp.where(
        active_mask, activation_gradient + sparsity_gradient, 0.0
    ).astype(jnp.bfloat16)
    enc_grad = jnp.einsum(
        "id,if->df",
        lax.all_gather(local_rows, "feat", axis=0, tiled=True),
        preactivation_gradient,
        preferred_element_type=jnp.float32,
    )
    loss_value = (squares_total + 2.0 * ERROR_SCALE * PENALTY_WEIGHT * penalty_total) / (
        lax.axis_size("layer") * token_count * local_rows.shape[1]
    )
    return (
        loss_value,
        recon.astype(jnp.bfloat16)[None],
        dec_grad[:, None],
        enc_grad.astype(jnp.bfloat16)[None],
    )


def solution(mesh):
    return jax.shard_map(
        body,
        mesh=mesh,
        in_specs=(
            P("layer", "feat", None),
            P("layer", None, "feat"),
            P("layer", "feat"),
            P(None, "layer", "feat", None),
            P("layer", "feat", None),
        ),
        out_specs=(
            P(),
            P("layer", "feat", None),
            P(None, "layer", "feat", None),
            P("layer", None, "feat"),
        ),
        check_vma=False,
    )
```

profile of v0, /device:TPU:1, one launch (start us, length us, event | category | flops | bytes accessed | tf_op | source)
XLA Modules:
  0.0 1679.2 jit_solution(8954540019723485133)
XLA Ops:
  7.2 0.0 all-gather.6.cloned.1.call-start
  7.2 1.4 copy.19
  8.7 0.0 all-reduce.4.cloned.1.call-start
  8.7 0.7 multiply_bitcast_fusion
  9.4 223.4 %all-gather.6.cloned.1.call-done = bf16[1,384,2304]{2,0,1:T(2,128)(2,1)} async-done(((bf16[1,3,2304]{2,0,1:T(2,128)(2,1)}), bf16[1,384,2304]{2,0,1:T(2,128)(2,1)}) %all-gather.6.cloned.1.call-update) | async-done | bytes 1769488 | tf_op jit(solution)/shard_map/all_gather | solution.py:15
  232.8 2.8 fusion.14
  235.6 14.4 all-gather.1
  250.1 2.5 convolution_bitcast_fusion
  252.6 0.0 all-reduce.4.cloned.1.call-update
  252.6 0.0 all-gather.8.cloned.1.call-start
  252.6 1.3 dynamic-slice
  254.6 1085.1 %all-reduce.4.cloned.1.call-done = f32[384,2304]{1,0:T(8,128)} async-done(((f32[384,2304]{1,0:T(8,128)}), f32[384,2304]{1,0:T(8,128)}) %all-reduce.4.cloned.1.call-update) | async-done | bytes 3538960
  1339.7 2.1 fusion.26
  1341.8 0.0 all-gather.8.cloned.1.call-update
  1341.8 0.0 reduce-scatter.2.cloned.1.call-start
  1341.9 215.0 %all-gather.8.cloned.1.call-done = bf16[128,3,2304]{2,1,0:T(4,128)(2,1)} async-done(((bf16[1,3,2304]{2,1,0:T(4,128)(2,1)}), bf16[128,3,2304]{2,1,0:T(4,128)(2,1)}) %all-gather.8.cloned.1.call-update) | async-done | bytes 1769488 | tf_op jit(solution)/shard_map/all_gather | solution.py:35
  1556.9 4.1 reshape.20
  1561.0 1.6 convolution_bitcast_fusion.1
  1562.5 0.0 reduce-scatter.2.cloned.1.call-update
  1562.5 0.6 broadcast_multiply_fusion
  1563.2 100.5 %all-reduce.1 = (f32[]{:T(128)}, f32[]{:T(128)}) all-reduce(f32[]{:T(128)} %get-tuple-element.25, f32[]{:T(128)} %get-tuple-element.27), channel_id=1, replica_groups=mesh['feat'=128,'layer'=4] {'feat','layer'}, use_global_device_ids=true, to_apply=%region_2.3 | all-reduce | flops 2 | bytes 16 | tf_op jit(solution)/shard_map/psum | solution.py:37
  1664.9 1.5 fusion.25
  1666.5 1.8 fusion
  1668.3 3.3 fusion.1
  (6 shorter events, 0.0 us)
Async XLA Ops:
  7.2 242.9 %copy-start = (bf16[4,1,64,2304]{3,2,1,0:T(8,128)(2,1)S(1)}, bf16[4,1,64,2304]{3,2,1,0:T(8,128)(2,1)}, u32[]{:S(2)}) copy-start(bf16[4,1,64,2304]{3,2,1,0:T(8,128)(2,1)} %param.8) | copy-start | bytes 3538948
  7.2 225.6 %all-gather.6.cloned.1.call-start = ((), (), s32[]{:S(2)}) async-start(), calls=%async_computation.2 | async-start | bytes 3566592 | tf_op jit(solution)/shard_map/all_gather | solution.py:15
  8.7 1331.0 %all-reduce.4.cloned.1.call-start = ((), (), s32[]{:S(2)}) async-start(), calls=%async_computation.4 | async-start | bytes 7077888
  252.6 1087.1 %copy-start.1 = (bf16[1,3,2304]{2,1,0:T(4,128)(2,1)S(1)}, bf16[1,3,2304]{2,1,0:T(4,128)(2,1)}, u32[]{:S(2)}) copy-start(bf16[1,3,2304]{2,1,0:T(4,128)(2,1)} %param.9) | copy-start | bytes 41476
  252.6 1304.3 %all-gather.8.cloned.1.call-start = ((), (), s32[]{:S(2)}) async-start(), calls=%async_computation.3 | async-start | bytes 2377728 | tf_op jit(solution)/shard_map/all_gather | solution.py:35
  1341.8 326.4 %reduce-scatter.2.cloned.1.call-start = ((), (), s32[]{:S(2)}) async-start(), calls=%async_computation.1 | async-start | bytes 491520 | tf_op jit(solution)/shard_map/reduce_scatter | solution.py:42
Sparse Core Ops, SparseCore 0:
  10.7 222.0 all-gather.5
  252.7 1086.9 all-reduce.3
  1342.4 214.4 all-gather.7
  1562.7 29.0 reduce-scatter.1
where the time goes:
time: 1680 us
  waiting for transfers between devices  1520 us (90%)
  blocking collectives  115 us (7%)
  between operations  16.9 us (1%)
    unnamed x5, waiting for transfers between devices  1090 us
    all_gather x1, waiting for transfers between devices, body(): lax.all_gather(local_rows, 'feat', axis=0, tiled=True)  223 us
    all_gather x1, waiting for transfers between devices, body(): grad_all = lax.all_gather(grad_local, 'feat', axis=0, tiled=True)  215 us
    psum x1, blocking collectives, body(): squares_total = lax.psum(squares_local, ('feat', 'layer'))  100 us
  transfers between devices with their start and end apart: 4, of which 3 were waited for; matrix products, arithmetic and copies ran while one was open for 0% of the time, Pallas kernels for 0%

commit v1 on v0

--- a/solution.py
+++ b/solution.py
@@ -32,7 +32,9 @@
     )
     error_rows = recon - target[0].astype(jnp.float32)
     grad_local = (error_rows / ERROR_SCALE).astype(jnp.bfloat16)
-    grad_all = lax.all_gather(grad_local, "feat", axis=0, tiled=True)
+    grad_all = jnp.concatenate(
+        lax.all_to_all(jnp.stack([grad_local] * lax.axis_size("feat")), "feat", 0, 0), axis=0
+    )
     squares_local = jnp.sum(error_rows * error_rows)
     squares_total = lax.psum(squares_local, ("feat", "layer"))
     dec_grad = jnp.einsum(

time: 1680 us -> 1530 us (0.911)
  waiting for transfers between devices: 1520 us -> 1310 us
  blocking collectives: 115 us -> 178 us
    all_gather x1 -> x0, waiting for transfers between devices: 215 us -> none  [body(): grad_all = lax.all_gather(grad_local, 'feat', axis=0, tiled=True)]
    all_to_all x0 -> x1, blocking collectives: none -> 64.9 us  [body(): lax.all_to_all(jnp.stack([grad_local] * lax.axis_size('feat')), 'feat', 0...]
    unnamed x5 -> x4, waiting for transfers between devices: 1090 us -> 1090 us
  transfers between devices with their start and end apart: 4 -> 3, of which waited for: 3 -> 2; matrix products, arithmetic and copies ran while one was open for 0% -> 0% of each run, Pallas kernels for 0% -> 0%
where the time goes in v1:
time: 1530 us
  waiting for transfers between devices  1310 us (86%)
  blocking collectives  178 us (12%)
  between operations  16.9 us (1%)
    unnamed x4, waiting for transfers between devices  1090 us
    all_gather x1, waiting for transfers between devices, body(): lax.all_gather(local_rows, 'feat', axis=0, tiled=True)  223 us
    psum x1, blocking collectives, body(): squares_total = lax.psum(squares_local, ('feat', 'layer'))  99.1 us
    all_to_all x1, blocking collectives, body(): lax.all_to_all(jnp.stack([grad_local] * lax.axis_size('feat')), 'feat', 0...  64.9 us
  transfers between devices with their start and end apart: 3, of which 2 were waited for; matrix products, arithmetic and copies ran while one was open for 0% of the time, Pallas kernels for 0%

profile of v1, /device:TPU:1, one launch (start us, length us, event | category | flops | bytes accessed | tf_op | source)
XLA Modules:
  0.0 1529.8 jit_solution(8850414569808949374)
XLA Ops:
  7.2 0.0 all-gather.4.cloned.1.call-start
  7.2 1.4 copy.19
  8.7 0.0 all-gather.4.cloned.1.call-update
  8.7 0.0 all-reduce.4.cloned.1.call-start
  8.7 0.7 multiply_bitcast_fusion
  9.4 223.4 %all-gather.4.cloned.1.call-done = bf16[1,384,2304]{2,0,1:T(2,128)(2,1)} async-done(((bf16[1,3,2304]{2,0,1:T(2,128)(2,1)}), bf16[1,384,2304]{2,0,1:T(2,128)(2,1)}) %all-gather.4.cloned.1.call-update) | async-done | bytes 1769488 | tf_op jit(solution)/shard_map/all_gather | solution.py:15
  232.8 3.4 fusion.14
  236.3 0.6 copy-done.4
  236.9 14.4 all-gather.1
  251.3 0.7 copy-done.2
  252.0 2.5 convolution_bitcast_fusion
  254.5 0.0 reduce-scatter.2.cloned.1.call-start
  254.6 1.3 dynamic-slice
  256.5 1085.1 %all-reduce.4.cloned.1.call-done = f32[384,2304]{1,0:T(8,128)} async-done(((f32[384,2304]{1,0:T(8,128)}), f32[384,2304]{1,0:T(8,128)}) %all-reduce.4.cloned.1.call-update) | async-done | bytes 3538960
  1341.6 1.5 multiply_convert_fusion
  1343.1 0.6 stack.2
  1343.8 64.9 %all_to_all.5 = bf16[128,3,2304]{2,1,0:T(4,128)(2,1)S(1)} all-to-all(bf16[128,3,2304]{2,1,0:T(4,128)(2,1)S(1)} %stack.2), channel_id=1, replica_groups=mesh['feat'=128,'layer'=4] {'feat'}, dimensions={0} | all-to-all | bytes 3538944 | tf_op jit(solution)/shard_map/all_to_all | solution.py:36
  1408.6 2.7 reshape.24
  1411.3 3.2 convolution_bitcast_fusion.1
  1414.6 0.6 broadcast_multiply_fusion
  1415.2 99.1 %all-reduce.1 = (f32[]{:T(128)}, f32[]{:T(128)}) all-reduce(f32[]{:T(128)} %get-tuple-element.25, f32[]{:T(128)} %get-tuple-element.27), channel_id=1, replica_groups=mesh['feat'=128,'layer'=4] {'feat','layer'}, use_global_device_ids=true, to_apply=%region_2.3 | all-reduce | flops 2 | bytes 16 | tf_op jit(solution)/shard_map/psum | solution.py:39
  1515.5 1.5 fusion.25
  1517.1 1.8 fusion
  1518.9 3.3 fusion.1
  (17 shorter events, 0.1 us)
Async XLA Ops:
  7.2 244.8 %copy-start = (bf16[4,1,64,2304]{3,2,1,0:T(8,128)(2,1)S(1)}, bf16[4,1,64,2304]{3,2,1,0:T(8,128)(2,1)}, u32[]{:S(2)}) copy-start(bf16[4,1,64,2304]{3,2,1,0:T(8,128)(2,1)} %param.8) | copy-start | bytes 3538948
  7.2 225.6 %all-gather.4.cloned.1.call-start = ((), (), s32[]{:S(2)}) async-start(), calls=%async_computation.3 | async-start | bytes 3566592 | tf_op jit(solution)/shard_map/all_gather | solution.py:15
  8.7 1332.9 %all-reduce.4.cloned.1.call-start = ((), (), s32[]{:S(2)}) async-start(), calls=%async_computation.4 | async-start | bytes 7077888
  236.3 0.6 copy-start.4
  251.3 0.7 copy-start.2
  254.5 1087.1 %copy-start.7 = (bf16[1,3,2304]{2,1,0:T(4,128)(2,1)S(1)}, bf16[1,3,2304]{2,1,0:T(4,128)(2,1)}, u32[]{:S(2)}) copy-start(bf16[1,3,2304]{2,1,0:T(4,128)(2,1)} %param.9) | copy-start | bytes 41476
  254.5 1264.4 %reduce-scatter.2.cloned.1.call-start = ((), (), s32[]{:S(2)}) async-start(), calls=%async_computation.2 | async-start | bytes 491520 | tf_op jit(solution)/shard_map/reduce_scatter | solution.py:44
  1411.3 105.8 %copy-start.1 = (bf16[384,2304,1]{1,0,2:T(8,128)(2,1)S(1)}, bf16[384,2304,1]{1,0,2:T(8,128)(2,1)}, u32[]{:S(2)}) copy-start(bf16[384,2304,1]{1,0,2:T(8,128)(2,1)} %reshape.24) | copy-start | bytes 5308420
  1411.3 105.8 %copy-start.3 = (bf16[1536,64]{0,1:T(8,128)(2,1)S(1)}, bf16[1536,64]{0,1:T(8,128)(2,1)}, u32[]{:S(2)}) copy-start(bf16[1536,64]{0,1:T(8,128)(2,1)} %copy-done.2) | copy-start | bytes 589828
  1414.5 104.3 %copy-start.5 = (bf16[384,64]{0,1:T(8,128)(2,1)S(1)}, bf16[384,64]{0,1:T(8,128)(2,1)}, u32[]{:S(2)}) copy-start(bf16[384,64]{0,1:T(8,128)(2,1)} %copy-done.4) | copy-start | bytes 147460
  1414.5 104.3 %copy-start.6 = (f32[384,64]{0,1:T(8,128)S(1)}, f32[384,64]{0,1:T(8,128)}, u32[]{:S(2)}) copy-start(f32[384,64]{0,1:T(8,128)} %get-tuple-element.28) | copy-start | bytes 294916
Sparse Core Ops, SparseCore 0:
  10.7 222.0 all-gather.3
  254.6 1086.9 all-reduce.3
  1414.7 25.4 reduce-scatter.1
